TPU v7x, 512 devices: a whole 4x4x16 slice. The times are simulated.
512 devices in a mesh: row: 16 (over y, z_hi), col: 32 (over x, z_lo, core).
Axes of the slice: x: 4, y: 4, z: 16 (z_hi: 4, z_lo: 4; z = z_hi * 4 + z_lo), core: 2. Of those that a mesh axis runs over, the one named last changes fastest.
Arguments:
- inv_known: float32 [8192, 8192], P('row', 'col'), as said below
- pattern: int32 [128, 128], P('row', 'col'), may hold values from 0 to 1, as said below
- factor: float32 [8192, 2, 512], P(('row', 'col')), may hold values from -0.0625 to 0.0625
- listed: int32 [8192, 2], P(('row', 'col')), may hold values 0 or 1
- diag_inverse: float32 [512, 2, 512], P('col'), may hold values from -6 to 6
Outputs:
- inverse_columns: float32 [512, 2, 8192], P('col', None, 'row')
- schur: float32 [512, 2, 512], P('col')
Inputs may be any that keep to these rules, and one draw needn't show every extreme that they name: `inv_known`: symmetric. `pattern`: symmetric; every diagonal tile is present.
All inputs are finite; a program needn't handle non-finite values. No bound on the sum of `listed` on one device may be relied on, other than what follows from the above.
Results may differ from a plain program's by a relative error of at most 0.0001.
Values sent between devices are 32-bit elements; how exact they have to be, the bound alone decides.
A program may use at most 64 MiB of HBM per device.

v0:
```python
import jax
import jax.numpy as jnp
from jax import lax
from jax.sharding import PartitionSpec as P


def in_one_piece(arrays, axis, dim, along):
    columns = [a.reshape(*a.shape[:along], -1) for a in arrays]
    both = jnp.concatenate(columns, axis=along)
    filled, at, finished = (lax.all_gather(both, axis, axis=dim, tiled=True), 0, [])
    for a, column in zip(arrays, columns):
        slab = filled[..., at : at + column.shape[along]]
        finished.append(slab.reshape(*slab.shape[:along], *a.shape[along:]))
        at += column.shape[along]
    return tuple(finished)


def in_blocks(x, dim, peers):
    before, after = (x.shape[:dim], x.shape[dim + 1 :])
    return jnp.moveaxis(x.reshape(*before, peers, -1, *after), dim, 0)


def sum_at_owner(x, axis, dim):
    parts = in_blocks(x, dim, lax.axis_size(axis))
    arrived = lax.all_to_all(parts, axis, split_axis=0, concat_axis=0, tiled=True)
    return arrived.sum(axis=0)


def from_everyone(x, axis):
    copies = jnp.broadcast_to(x, (lax.axis_size(axis), *x.shape))
    return lax.all_to_all(copies, axis, split_axis=0, concat_axis=0, tiled=True)


def of_everyone(x, axis):
    everything = from_everyone(x, axis)
    return jnp.sum(everything, axis=0)


def supernode_pass(present, masked, listed_f, diag_part, ratio):
    row_block, row_listed = in_one_piece((masked, listed_f), "col", 0, 2)
    held = sum_at_owner(
        jnp.einsum("ij,ika->jka", present, row_block, precision=lax.Precision.HIGHEST), "row", 0
    )
    count_row = lax.axis_size("row")
    count_col = lax.axis_size("col")
    local_rows = held.shape[0]
    nodes = held.shape[1]
    narrow = held.shape[2] // count_col
    by_column = lax.all_to_all(held[None], "col", split_axis=3, concat_axis=0, tiled=True)
    grouped = by_column.reshape(count_row, 1, ratio, local_rows, nodes, narrow)
    moved = lax.all_to_all(grouped, "row", split_axis=0, concat_axis=1, tiled=True)
    ordered = jnp.transpose(moved[0], (1, 0, 2, 3, 4)).reshape(
        ratio * count_row * local_rows, nodes, narrow
    )
    summed = jnp.transpose(ordered, (2, 1, 0))
    columns = -summed * jnp.transpose(row_listed)[None, :, :]
    update = jnp.einsum("akj,jkb->akb", columns, row_block, precision=lax.Precision.HIGHEST)
    schur = diag_part - of_everyone(update, "row")
    return (columns, schur)


def local(inv_known, pattern, factor, listed, diag_inverse):
    tile = inv_known.shape[0] // pattern.shape[0]
    flags = pattern.astype(jnp.float32)
    spread = jnp.repeat(jnp.repeat(flags, tile, axis=0), tile, axis=1)
    present = inv_known * spread
    listed_f = listed.astype(jnp.float32)
    masked = factor * listed_f[:, :, None]
    ratio = lax.axis_size("col") // lax.axis_size("row")
    columns, schur = supernode_pass(present, masked, listed_f, diag_inverse, ratio)
    return (columns, schur)


def solution(mesh):
    in_specs = (
        P("row", "col"),
        P("row", "col"),
        P(("row", "col"), None, None),
        P(("row", "col"), None),
        P("col", None, None),
    )
    out_specs = (P("col", None, "row"), P("col", None, None))
    return jax.shard_map(local, mesh=mesh, in_specs=in_specs, out_specs=out_specs, check_vma=False)
```

profile of v0, /device:TPU:32, one launch (start us, length us, event | category | flops | bytes accessed | tf_op | source)
XLA Modules:
  0.0 265.9 jit_solution(16687229242903270589)
XLA Ops:
  7.2 0.7 fusion.8
  7.9 0.1 copy.49
  8.0 0.9 copy_multiply_fusion
  8.9 0.6 pad_maximum_fusion
  9.6 1.2 copy.47
  10.8 0.7 convert_element_type.6
  11.7 67.7 %all-gather.2.cloned.1.call-done = f32[512,2,513]{2,0,1:T(8,128)} async-done(((f32[16,2,513]{2,0,1:T(8,128)}), f32[512,2,513]{2,0,1:T(8,128)}) %all-gather.2.cloned.1.call-update) | async-done | bytes 2101264 | tf_op jit(solution)/shard_map/all_gather | solution.py:10
  79.4 3.5 %fusion.2 = f32[256,2,512]{2,0,1:T(8,128)S(1)} fusion(f32[512,2,513]{2,0,1:T(8,128)} %all-gather.2.cloned.1.call-done, f32[512,256]{0,1:T(8,128)S(1)} %bitcast_multiply_fusion), kind=kOutput, calls=%fused_computation.2 | convolution fusion | flops 1610612736 | bytes 3670016 | tf_op jit(solution)/shard_map/ij,ika->jka/dot_general | solution.py:42
  83.0 66.8 %all_to_all.34 = f32[16,16,2,512]{3,1,2,0:T(8,128)S(1)} all-to-all(f32[16,16,2,512]{3,1,2,0:T(8,128)S(1)} %copy.50), channel_id=1, replica_groups=mesh['row'=16,'col'=32] {'row'}, dimensions={0} | all-to-all | bytes 2097152 | tf_op jit(solution)/shard_map/all_to_all | solution.py:25
  149.8 0.2 copy.51
  150.1 0.7 reshape.37
  150.8 15.7 %all_to_all.35 = f32[32,1,512]{2,1,0:T(1,128)S(1)} all-to-all(f32[32,1,512]{2,1,0:T(1,128)S(1)} %reshape.37), channel_id=1, replica_groups=mesh['row'=16,'col'=32] {'col'}, dimensions={0} | all-to-all | bytes 131072 | tf_op jit(solution)/shard_map/all_to_all | solution.py:49
  166.5 0.5 broadcast.3
  167.0 0.8 reduce.2
  167.8 0.7 reshape.38
  168.5 1.2 copy.59
  169.8 1.3 copy.65
  171.1 0.9 reshape.39
  172.0 3.5 %all-to-all-start.2 = ((f32[16,1,1024]{2,1,0:T(1,128)}), f32[16,1,1024]{2,1,0:T(1,128)S(1)}, u32[]{:S(2)}, u32[]{:S(2)}) async-start(f32[16,1,1024]{2,1,0:T(1,128)} %reshape.39), calls=%async_computation.2 | async-start | bytes 131072 | tf_op jit(solution)/shard_map/all_to_all | solution.py:51
  175.5 0.2 slice_reduce_fusion
  175.7 16.0 %all-to-all-done.2 = f32[16,1,1024]{2,1,0:T(1,128)S(1)} async-done(((f32[16,1,1024]{2,1,0:T(1,128)}), f32[16,1,1024]{2,1,0:T(1,128)S(1)}, u32[]{:S(2)}, u32[]{:S(2)}) %all-to-all-start.2) | async-done | bytes 65568 | tf_op jit(solution)/shard_map/all_to_all | solution.py:51
  191.8 0.8 reduce.3
  192.6 0.2 reshape.40
  192.8 0.8 negate_bitcast_fusion
  193.6 1.5 copy.55
  195.1 0.3 neg.18
  195.4 1.2 fusion.4
  196.6 1.1 broadcast_in_dim.20
  197.7 3.7 %all-to-all-start.3 = ((f32[16,16,2,512]{3,1,2,0:T(8,128)}), f32[16,16,2,512]{3,1,2,0:T(8,128)S(1)}, u32[]{:S(2)}, u32[]{:S(2)}) async-start(f32[16,16,2,512]{3,1,2,0:T(8,128)} %broadcast_in_dim.20), calls=%async_computation.3 | async-start | bytes 2097152 | tf_op jit(solution)/shard_map/all_to_all | solution.py:31
  201.4 0.7 copy.57
  202.0 56.3 %all-to-all-done.3 = f32[16,16,2,512]{3,1,2,0:T(8,128)S(1)} async-done(((f32[16,16,2,512]{3,1,2,0:T(8,128)}), f32[16,16,2,512]{3,1,2,0:T(8,128)S(1)}, u32[]{:S(2)}, u32[]{:S(2)}) %all-to-all-start.3) | async-done | bytes 1048608 | tf_op jit(solution)/shard_map/all_to_all | solution.py:31
  258.4 0.7 copy.58
  (14 shorter events, 0.5 us)
Async XLA Ops:
  7.2 72.3 %all-gather.2.cloned.1.call-start = ((), (), s32[]{:S(2)}) async-start(), calls=%async_computation.4 | async-start | bytes 2703360 | tf_op jit(solution)/shard_map/all_gather | solution.py:10
  149.8 25.7 %copy-start = (f32[512,2,513]{2,0,1:T(8,128)S(1)}, f32[512,2,513]{2,0,1:T(8,128)}, u32[]{:S(2)}) copy-start(f32[512,2,513]{2,0,1:T(8,128)} %all-gather.2.cloned.1.call-done) | copy-start | bytes 6303748
  172.0 19.8 %all-to-all-start.2 = ((f32[16,1,1024]{2,1,0:T(1,128)}), f32[16,1,1024]{2,1,0:T(1,128)S(1)}, u32[]{:S(2)}, u32[]{:S(2)}) async-start(f32[16,1,1024]{2,1,0:T(1,128)} %reshape.39), calls=%async_computation.2 | async-start | bytes 131072 | tf_op jit(solution)/shard_map/all_to_all | solution.py:51
  196.6 61.8 %copy-start.1 = (f32[16,2,512]{2,1,0:T(2,128)S(1)}, f32[16,2,512]{2,1,0:T(2,128)}, u32[]{:S(2)}) copy-start(f32[16,2,512]{2,1,0:T(2,128)} %param.9) | copy-start | bytes 196612
  197.7 60.6 %all-to-all-start.3 = ((f32[16,16,2,512]{3,1,2,0:T(8,128)}), f32[16,16,2,512]{3,1,2,0:T(8,128)S(1)}, u32[]{:S(2)}, u32[]{:S(2)}) async-start(f32[16,16,2,512]{3,1,2,0:T(8,128)} %broadcast_in_dim.20), calls=%async_computation.3 | async-start | bytes 2097152 | tf_op jit(solution)/shard_map/all_to_all | solution.py:31
Sparse Core Ops, SparseCore 0:
  10.1 69.3 all-gather.1
where the time goes:
time: 267 us; the launch traced here: 266 us
  waiting for transfers between devices  140 us (52%)
  blocking collectives  82.5 us (31%)
  between operations  14.2 us (5%)
  local copies, waits for them, and re-layouts  11.8 us (4%)
  starting transfers between devices  7.2 us (3%)
  other arithmetic  5.58 us (2%)
  matrix products  4.68 us (2%)
    all_gather x1, waiting for transfers between devices, in_one_piece(): lax.all_gather(both, axis, axis=dim, tiled=True)  67.7 us
    all_to_all x1, blocking collectives, sum_at_owner(): lax.all_to_all(parts, axis, split_axis=0, concat_axis=0, tiled=True)  66.8 us
    all_to_all x1, waiting for transfers between devices, from_everyone(): return lax.all_to_all(copies, axis, split_axis=0, concat_axis=0, tiled=True)  56.3 us
    all_to_all x1, waiting for transfers between devices, supernode_pass(): lax.all_to_all(grouped, 'row', split_axis=0, concat_axis=1, tiled=True)  16 us
    all_to_all x1, blocking collectives, supernode_pass(): lax.all_to_all(held[None], 'col', split_axis=3, concat_axis=0, tiled=True)  15.7 us
  transfers between devices with their start and end apart: 3, of which 3 were waited for; matrix products, arithmetic and copies ran while one was open for 1% of the time, Pallas kernels for 0%

commit v1 on v0

v1 whole, which is shorter than its diff:
```python
import jax
import jax.numpy as jnp
from jax import lax
from jax.experimental import pallas as pl
from jax.experimental.pallas import tpu as pltpu
from jax.sharding import PartitionSpec as P

MESH = pl.DeviceIdType.MESH
F32 = jnp.float32
BF16 = jnp.bfloat16

S = 4
ROWS = 16
KS = 2
LANES = 128
GR = S * ROWS + 8


def mod(v):
    return lax.rem(v, S)


def split(v):
    hi = v.astype(BF16)
    return hi, (v - hi.astype(F32)).astype(BF16)


def dot3(ah, al, bh, bl):
    def dot(a, b):
        return jnp.dot(a, b, preferred_element_type=F32)

    return dot(ah, bh) + (dot(ah, bl) + dot(al, bh))


def kernel(
    inv_ref, pat_ref, fac_ref, lst_ref, dia_ref, col_ref, sch_ref,
    ph, plo, gat, mh, ml, tq, yb, zt, rb, ub, yu, zv, fw,
    g_send, g_recv, y_send, y_recv, z_send, z_recv,
    u_send, u_recv, v_send, v_recv, w_send, w_recv,
):
    r, c = lax.axis_index("row"), lax.axis_index("col")
    y, h = lax.div(r, S), lax.rem(r, S)
    x, z, core = lax.div(c, 2 * S), lax.rem(lax.div(c, 2), S), lax.rem(c, 2)
    sib = 1 - core

    def rid(yy, hh):
        return yy * S + hh

    def cid(xx, zz, cc):
        return (xx * S + zz) * 2 + cc

    def quarter(xx, yy):
        return mod(2 * xx + S - yy)

    mine = quarter(x, y)
    alone = jnp.logical_and(x == y, z == h)

    barrier = pltpu.get_barrier_semaphore()

    def greet(rr, cc):
        pl.semaphore_signal(barrier, inc=1, device_id=(rr, cc), device_id_type=MESH)

    greet(r, cid(x, z, sib))
    for d in (1, 2, 3):
        greet(r, cid(x, mod(z + d), core))
        greet(rid(mod(y + d), h), c)
        greet(rid(y, mod(h + d)), c)
    greet(r, cid(mod(x + 1), z, core))
    greet(r, cid(mod(x + 3), z, core))
    for hs in range(S):
        for cs in range(2):
            rr, cc = rid(quarter(y, x), hs), cid(y, h, cs)

            @pl.when(jnp.logical_or(rr != r, cc != c))
            def _():
                greet(rr, cc)

    listed = lst_ref[...].astype(F32)
    lane = lax.broadcasted_iota(jnp.int32, (ROWS, LANES), 1)
    row = lax.broadcasted_iota(jnp.int32, (ROWS, LANES), 0)
    spot = lane == row + lax.rem(c, LANES // ROWS) * ROWS
    for k in range(KS):
        flag = listed[:, k : k + 1]
        rows = fac_ref[:, k, :] * flag
        for b in range(S):
            gat[c, k, b * ROWS : (b + 1) * ROWS, :] = rows[:, b * LANES : (b + 1) * LANES]
        line = jnp.sum(jnp.where(spot, flag, 0.0), axis=0, keepdims=True)
        gat[c, k, S * ROWS :, :] = jnp.broadcast_to(line, (8, LANES))

    flags = pat_ref[...].astype(F32)
    tcol = lax.div(lax.broadcasted_iota(jnp.int32, (8, 256), 1), 64)
    wide = jnp.zeros((8, 256), F32)
    for t in range(4):
        wide = jnp.where(tcol == t, flags[:, t : t + 1], wide)
    for g in range(4):
        block = jnp.concatenate(
            [inv_ref[(2 * g + e) * 64 : (2 * g + e + 1) * 64, :] * wide[2 * g + e : 2 * g + e + 1, :] for e in range(2)],
            axis=0,
        )
        hi, lo = split(block.T)
        ph[:, g * 128 : (g + 1) * 128] = hi
        plo[:, g * 128 : (g + 1) * 128] = lo

    pl.semaphore_wait(barrier, 20 - alone.astype(jnp.int32))

    sends = []

    def send(src, dst, ssem, rsem, rr, cc):
        copy = pltpu.make_async_remote_copy(
            src_ref=src, dst_ref=dst, send_sem=ssem, recv_sem=rsem, device_id=(rr, cc), device_id_type=MESH
        )
        copy.start()
        sends.append(copy)

    def arrive(dst, rsem):
        pltpu.make_async_copy(dst, dst, rsem).wait()

    count = [0] * KS

    def pass_on(k, cs, cc):
        shard = gat.at[cs, k]
        send(shard, shard, g_send.at[k, count[k]], g_recv.at[k, cs], r, cc)
        count[k] += 1

    def got(k, cs):
        arrive(gat.at[cs, k], g_recv.at[k, cs])

    right, left = cid(mod(x + 1), z, core), cid(mod(x + 3), z, core)
    partner = cid(x, z, sib)

    def start_gather(k):
        for cc in (right, left, cid(x, mod(z + 1), core), cid(x, mod(z + 3), core), cid(x, mod(z + 2), core), partner):
            pass_on(k, c, cc)

    def line_gather(k):
        got(k, left)
        pass_on(k, left, right)
        pass_on(k, left, partner)
        got(k, right)
        pass_on(k, right, partner)
        for d in (1, 3, 2):
            cs = cid(x, mod(z + d), core)
            got(k, cs)
            for cc in (right, left, partner):
                pass_on(k, cs, cc)

    def finish_gather(k):
        for d in (1, 3, 2):
            cs = cid(mod(x + 3), mod(z + d), core)
            got(k, cs)
            if d == 1:
                pass_on(k, cs, right)
            pass_on(k, cs, partner)
            cs = cid(mod(x + 1), mod(z + d), core)
            got(k, cs)
            if d != 1:
                pass_on(k, cs, left)
            pass_on(k, cs, partner)
        for d in range(S):
            cs = cid(mod(x + 2), mod(z + d), core)
            got(k, cs)
            pass_on(k, cs, partner)
        for xx in range(S):
            for zz in range(S):
                got(k, cid(xx, zz, sib))

    def product(k):
        for b in range(0, S, 2):
            block = jnp.concatenate(
                [gat[:, k, e * ROWS : (e + 1) * ROWS, :].reshape(32 * ROWS, LANES) for e in (b, b + 1)], axis=1
            )
            bh, bl = split(block)
            mh[k, :, b * LANES : (b + 2) * LANES] = bh
            ml[k, :, b * LANES : (b + 2) * LANES] = bl
            t = dot3(ph[...], plo[...], bh, bl)
            tq[k, b] = t[:, :LANES]
            tq[k, b + 1] = t[:, LANES:]
        for d in (1, 3, 2):
            yy = mod(y + d)
            send(tq.at[k, quarter(x, yy)], yb.at[k, d], y_send.at[k, d], y_recv.at[k, d], rid(yy, h), c)

    def to_owner(k):
        for d in (1, 3, 2):
            arrive(yb.at[k, d], y_recv.at[k, d])
        total = (tq[k, mine] + yb[k, 1]) + (yb[k, 2] + yb[k, 3])
        zt[k] = total.T.reshape(8, ROWS, 256)
        for t in range(S):
            for cc in range(2):
                rr, ct, e = rid(x, z), cid(mine, t, cc), t * 2 + cc
                here = jnp.logical_and(rr == r, ct == c)

                @pl.when(here)
                def _():
                    pltpu.make_async_copy(zt.at[k, e], rb.at[k, h, core], z_recv.at[k, h, core]).start()

                @pl.when(jnp.logical_not(here))
                def _():
                    pltpu.make_async_remote_copy(
                        src_ref=zt.at[k, e], dst_ref=rb.at[k, h, core], send_sem=z_send.at[k, e],
                        recv_sem=z_recv.at[k, h, core], device_id=(rr, ct), device_id_type=MESH,
                    ).start()

    def sent_to_owner(k):
        for t in range(S):
            for cc in range(2):
                rr, ct, e = rid(x, z), cid(mine, t, cc), t * 2 + cc

                @pl.when(jnp.logical_or(rr != r, ct != c))
                def _():
                    pltpu.make_async_copy(zt.at[k, e], zt.at[k, e], z_send.at[k, e]).wait()

    def update(k):
        for hs in range(S):
            for cs in range(2):
                arrive(rb.at[k, hs, cs], z_recv.at[k, hs, cs])
        parts = rb[k]
        total = (parts[0] + parts[1]) + (parts[2] + parts[3])
        total = jnp.concatenate([total[0], total[1]], axis=1)
        line = jnp.concatenate(
            [jnp.sum(gat[8 * b : 8 * b + 8, k, S * ROWS :, :], axis=0)[0:1, :] for b in range(S)], axis=1
        )
        columns = -total * line
        col_ref[:, k, :] = columns
        ch, cl = split(columns)
        u = dot3(ch, cl, mh[k], ml[k])
        for q in range(S):
            ub[k, q] = u[:, q * LANES : (q + 1) * LANES]
        for d in (1, 3, 2):
            yy = mod(y + d)
            send(ub.at[k, yy], yu.at[k, d], u_send.at[k, d], u_recv.at[k, d], rid(yy, h), c)

    def across(k):
        for d in (1, 3, 2):
            arrive(yu.at[k, d], u_recv.at[k, d])
        zv[k, h] = (ub[k, y] + yu[k, 1]) + (yu[k, 2] + yu[k, 3])
        for d in (2, 1, 3):
            send(zv.at[k, h], zv.at[k, h], v_send.at[k, d], v_recv.at[k, d], rid(y, mod(h + d)), c)

    def back(k):
        for d in (1, 3, 2):
            hs = mod(h + S - d)
            arrive(zv.at[k, hs], v_recv.at[k, d])
        fw[k, y] = (zv[k, 0] + zv[k, 1]) + (zv[k, 2] + zv[k, 3])
        for d in (2, 1, 3):
            send(fw.at[k, y], fw.at[k, y], w_send.at[k, d], w_recv.at[k, d], rid(mod(y + d), h), c)

    def finish(k):
        for d in (1, 3, 2):
            ys = mod(y + S - d)
            arrive(fw.at[k, ys], w_recv.at[k, d])
        for q in range(S):
            at = slice(q * LANES, (q + 1) * LANES)
            sch_ref[:, k, at] = dia_ref[:, k, at] - fw[k, q]

    start_gather(0)
    line_gather(0)
    start_gather(1)
    finish_gather(0)
    product(0)
    line_gather(1)
    finish_gather(1)
    product(1)
    to_owner(0)
    to_owner(1)
    update(0)
    across(0)
    update(1)
    across(1)
    back(0)
    back(1)
    finish(0)
    finish(1)
    for copy in sends:
        copy.wait_send()
    sent_to_owner(0)
    sent_to_owner(1)


def local(inv_known, pattern, factor, listed, diag_inverse):
    width = diag_inverse.shape[0]
    vmem = pl.BlockSpec(memory_space=pltpu.VMEM)
    dma = pltpu.SemaphoreType.DMA
    out = jax.ShapeDtypeStruct((width, KS, 512), F32)
    return pl.pallas_call(
        kernel,
        out_shape=(out, out),
        in_specs=[vmem] * 5,
        out_specs=(vmem, vmem),
        scratch_shapes=[
            pltpu.VMEM((256, 512), BF16),
            pltpu.VMEM((256, 512), BF16),
            pltpu.VMEM((32, KS, GR, LANES), F32),
            pltpu.VMEM((KS, 512, 512), BF16),
            pltpu.VMEM((KS, 512, 512), BF16),
            pltpu.VMEM((KS, S, 256, LANES), F32),
            pltpu.VMEM((KS, S, 256, LANES), F32),
            pltpu.VMEM((KS, 8, ROWS, 256), F32),
            pltpu.VMEM((KS, S, 2, ROWS, 256), F32),
            pltpu.VMEM((KS, S, ROWS, LANES), F32),
            pltpu.VMEM((KS, S, ROWS, LANES), F32),
            pltpu.VMEM((KS, S, ROWS, LANES), F32),
            pltpu.VMEM((KS, S, ROWS, LANES), F32),
            dma((KS, 31)), dma((KS, 32)),
            dma((KS, S)), dma((KS, S)),
            dma((KS, 8)), dma((KS, S, 2)),
            dma((KS, S)), dma((KS, S)),
            dma((KS, S)), dma((KS, S)),
            dma((KS, S)), dma((KS, S)),
        ],
        compiler_params=pltpu.CompilerParams(collective_id=0, has_side_effects=True),
    )(inv_known, pattern, factor, listed, diag_inverse)


def solution(mesh):
    in_specs = (
        P("row", "col"),
        P("row", "col"),
        P(("row", "col"), None, None),
        P(("row", "col"), None),
        P("col", None, None),
    )
    out_specs = (P("col", None, "row"), P("col", None, None))
    return jax.shard_map(local, mesh=mesh, in_specs=in_specs, out_specs=out_specs, check_vma=False)
```

time: 267 us -> 88.2 us (0.33)
  the two profiles are of different devices: /device:TPU:32 before, /device:TPU:72 now
where the time goes in v1:
time: 88.2 us; the launch traced here: 88 us
  Pallas kernels  83.2 us (94%)
  local copies, waits for them, and re-layouts  4.18 us (5%)
    pallas_call x1, Pallas kernels, local(): pl.pallas_call(kernel, out_shape=(out, out), in_specs=[vmem] * 5, out_spe...  83.2 us
    unnamed x8, local copies, waits for them, and re-layouts  4.18 us

profile of v1, /device:TPU:72, one launch (start us, length us, event | category | flops | bytes accessed | tf_op | source)
XLA Modules:
  0.0 88.0 jit_solution(5486615901618764063)
XLA Ops:
  0.6 0.0 copy-start.1
  0.6 1.4 %copy.7.pat_ref = s32[8,4]{1,0:T(8,128)} copy(s32[8,4]{0,1:T(4,128)} %param.6) | data formatting | bytes 256 | tf_op args[1]
  2.0 0.0 copy-done.1
  2.0 0.7 copy.8.lst_ref
  2.7 83.2 %shard_map.68 = (f32[16,2,512]{2,1,0:T(2,128)}, f32[16,2,512]{2,1,0:T(2,128)}) custom-call(f32[512,256]{1,0:T(8,128)} %inv_ref.1, s32[8,4]{1,0:T(8,128)} %copy.7.pat_ref, f32[16,2,512]{2,1,0:T(2,128)} %fac_ref.1, s32[16,2]{1,0:T(8,128)} %copy.8.lst_ref, f32[16,2,512]{2,1,0:T(2,128)} %dia_ref.1), custom_call_target="tpu_custom_call" | custom-call | tf_op jit(solution)/shard_map/pallas_call | solution.py:284
  85.8 0.0 copy-start
  85.8 1.5 %copy.11 = f32[16,2,512]{2,1,0:T(2,128)} copy(f32[16,2,512]{2,1,0:T(2,128)} %get-tuple-element.4) | data formatting | bytes 131072
  87.3 0.0 copy-done
  87.4 0.6 copy.12
Async XLA Ops:
  0.6 1.4 %copy-start.1 = (s32[16,2]{0,1:T(2,128)S(1)}, s32[16,2]{0,1:T(2,128)}, u32[]{:S(2)}) copy-start(s32[16,2]{0,1:T(2,128)} %param.8) | copy-start | bytes 388
  85.8 1.5 %copy-start = (f32[16,2,512]{2,1,0:T(2,128)S(1)}, f32[16,2,512]{2,1,0:T(2,128)}, u32[]{:S(2)}) copy-start(f32[16,2,512]{2,1,0:T(2,128)} %get-tuple-element.5) | copy-start | bytes 196612

commit v2 on v1

v2 whole, which is shorter than its diff:
```python
import jax
import jax.numpy as jnp
from jax import lax
from jax.experimental import pallas as pl
from jax.experimental.pallas import tpu as pltpu
from jax.sharding import PartitionSpec as P

MESH = pl.DeviceIdType.MESH
F32 = jnp.float32
BF16 = jnp.bfloat16

S = 4
ROWS = 16
KS = 2
LANES = 128
PART = 32
CHUNKS = 4
HEAD = 8
GR = HEAD + CHUNKS * 2 * ROWS


def mod(v):
    return lax.rem(v, S)


def split(v):
    hi = v.astype(BF16)
    return hi, (v - hi.astype(F32)).astype(BF16)


def dot3(ah, al, bh, bl):
    def dot(a, b):
        return jnp.dot(a, b, preferred_element_type=F32)

    return dot(ah, bh) + (dot(ah, bl) + dot(al, bh))


def regroup(v):
    blocks = []
    for t in range(S):
        blocks += [v[:, q * LANES + t * PART : q * LANES + (t + 1) * PART] for q in range(S)]
    return jnp.concatenate(blocks, axis=1)


def kernel(
    inv_ref, pat_ref, fac_ref, lst_ref, col_ref, sch_ref,
    inv, ph, plo, gat, mh, ml, tq, yb, zt, rb, ub, yu, zv, fw,
    i_sem, far_sem, g_send, g_recv, y_send, y_recv, z_send, z_recv,
    u_send, u_recv, v_send, v_recv, w_send, w_recv,
):
    r, c = lax.axis_index("row"), lax.axis_index("col")
    y, h = lax.div(r, S), lax.rem(r, S)
    x, z, core = lax.div(c, 2 * S), lax.rem(lax.div(c, 2), S), lax.rem(c, 2)
    sib = 1 - core

    def rid(yy, hh):
        return yy * S + hh

    def cid(xx, zz, cc):
        return (xx * S + zz) * 2 + cc

    def quarter(xx, yy):
        return mod(2 * xx + S - yy)

    mine = quarter(x, y)
    line = (z + 1 - 2 * lax.rem(z, 2), jnp.where(z < 2, 2, 1), jnp.where(z < 2, 3, 0))
    right, left, partner = cid(mod(x + 1), z, core), cid(mod(x + 3), z, core), cid(x, z, sib)
    across_x = cid(mod(x + 2), z, core)

    barrier = pltpu.get_barrier_semaphore()

    def greet(sem, rr, cc):
        pl.semaphore_signal(sem, inc=1, device_id=(rr, cc), device_id_type=MESH)

    greet(barrier, rid(y, mod(h + 1)), c)
    greet(barrier, rid(y, mod(h + 3)), c)
    for zz in line:
        greet(barrier, r, cid(x, zz, core))
    for d in (2, 1, 3):
        greet(barrier, rid(mod(y + d), h), c)
    for cc in (right, left, across_x, partner):
        greet(barrier, r, cc)

    load = pltpu.make_async_copy(inv_ref, inv, i_sem)
    load.start()

    listed = lst_ref[...].astype(F32)
    eye = lax.broadcasted_iota(jnp.int32, (ROWS, ROWS), 0) == lax.broadcasted_iota(jnp.int32, (ROWS, ROWS), 1)
    lane = lax.broadcasted_iota(jnp.int32, (ROWS, LANES), 1)
    row = lax.broadcasted_iota(jnp.int32, (ROWS, LANES), 0)
    spot = lane == row + lax.rem(c, LANES // ROWS) * ROWS
    lines = []
    for k in range(KS):
        flag = jnp.sum(jnp.where(eye, listed[k : k + 1, :], 0.0), axis=1, keepdims=True)
        rows = regroup(fac_ref[:, k, :] * flag)
        for t in range(S):
            at = HEAD + (k * S + t) * ROWS
            gat[c, at : at + ROWS, :] = rows[:, t * LANES : (t + 1) * LANES]
        lines.append(jnp.sum(jnp.where(spot, flag, 0.0), axis=0, keepdims=True))
    which = lax.broadcasted_iota(jnp.int32, (HEAD, LANES), 0) == 0
    gat[c, :HEAD, :] = jnp.where(which, lines[0], lines[1])

    pl.semaphore_wait(barrier, 12)

    rounds = (
        [(rid(y, mod(h + 1)), c), (rid(y, mod(h + 3)), c)],
        [(rid(mod(y + d), h), c) for d in (2, 1, 3)],
        [(r, cid(x, zz, core)) for zz in line],
        [(r, right), (r, left), (r, across_x)],
        [(r, partner)],
    )

    def tell(n):
        for rr, cc in rounds[n]:
            greet(far_sem.at[n], rr, cc)

    def heard(n):
        pl.semaphore_wait(far_sem.at[n], len(rounds[n]))
        if n + 1 < len(rounds):
            tell(n + 1)

    tell(0)

    sends = []

    def copy(src, dst, ssem, rsem, rr, cc):
        return pltpu.make_async_remote_copy(
            src_ref=src, dst_ref=dst, send_sem=ssem, recv_sem=rsem, device_id=(rr, cc), device_id_type=MESH
        )

    def send(*args):
        it = copy(*args)
        it.start()
        sends.append(it)

    def arrive(dst, sem):
        pltpu.make_async_copy(dst, dst, sem).wait()

    def span(n):
        first = 0 if n == 0 else HEAD + n * 2 * ROWS
        return pl.ds(first, HEAD + (n + 1) * 2 * ROWS - first)

    def pass_on(n, cs, *to):
        shard = gat.at[cs, span(n)]
        for cc in to:
            copy(shard, shard, g_send.at[n], g_recv.at[n, cs], r, cc).start()

    def got(n, cs):
        arrive(gat.at[cs, span(n)], g_recv.at[n, cs])

    def start_gather(n):
        pass_on(n, c, right, left, cid(x, line[2], core), cid(x, line[1], core), cid(x, line[0], core), partner)

    def line_gather(n):
        got(n, left)
        pass_on(n, left, right, partner)
        got(n, right)
        pass_on(n, right, partner)
        for zz in line:
            cs = cid(x, zz, core)
            got(n, cs)
            pass_on(n, cs, right, left, partner)

    def relay_gather(n):
        for e, zz in enumerate(line):
            cs = cid(mod(x + 3), zz, core)
            got(n, cs)
            if e == 0:
                pass_on(n, cs, right)
            pass_on(n, cs, partner)
            cs = cid(mod(x + 1), zz, core)
            got(n, cs)
            if e != 0:
                pass_on(n, cs, left)
            pass_on(n, cs, partner)

    def finish_gather(n):
        for zz in (z, *line):
            cs = cid(mod(x + 2), zz, core)
            got(n, cs)
            pass_on(n, cs, partner)
        for cs in range(S * S):
            got(n, 2 * cs + sib)

    def gathered(n):
        shards = gat.at[pl.ds(0, 31), span(n)]
        pltpu.make_async_copy(shards, shards, g_send.at[n]).wait()

    def prepare():
        flags = pat_ref[...].astype(F32)
        tile = lax.div(lax.broadcasted_iota(jnp.int32, (S, 512), 1), 64)
        wide = jnp.zeros((S, 512), F32)
        for e in range(8):
            wide = jnp.where(tile == e, flags[:, e : e + 1], wide)
        load.wait()
        for g in range(4):
            at = slice(g * LANES, (g + 1) * LANES)
            mask = jnp.concatenate([jnp.broadcast_to(wide[t : t + 1, at], (64, LANES)) for t in range(S)], axis=0)
            hi, lo = split(inv[at, :].T * mask)
            ph[:, at] = hi
            plo[:, at] = lo

    def product(n):
        k, p = n // 2, n % 2
        at = HEAD + n * 2 * ROWS
        block = jnp.concatenate(
            [gat[:, at + e * ROWS : at + (e + 1) * ROWS, :].reshape(32 * ROWS, LANES) for e in range(2)], axis=1
        )
        bh, bl = split(block)
        mh[k, :, p * 256 : (p + 1) * 256] = bh
        ml[k, :, p * 256 : (p + 1) * 256] = bl
        t = dot3(ph[...], plo[...], bh, bl).T
        for e in range(2):
            for q in range(S):
                at = (e * S + q) * PART
                tq[n, q, e] = t[at : at + PART]
        for d in (2, 1, 3):
            yy = mod(y + d)
            send(tq.at[n, quarter(x, yy)], yb.at[n, d], y_send.at[n, d], y_recv.at[n, d], rid(yy, h), c)

    def owners(n):
        for e in range(2):
            for cc in range(2):
                yield e * 2 + cc, rid(x, z), cid(mine, (n % 2) * 2 + e, cc)

    def to_owner(n):
        k = n // 2
        for d in (1, 3, 2):
            arrive(yb.at[n, d], y_recv.at[n, d])
        total = (tq[n, mine] + yb[n, 1]) + (yb[n, 2] + yb[n, 3])
        zt[n] = total.reshape(4, ROWS, 256)
        for e, rr, ct in owners(n):
            here = jnp.logical_and(rr == r, ct == c)

            @pl.when(here)
            def _():
                pltpu.make_async_copy(zt.at[n, e], rb.at[k, h, core], z_recv.at[k, h, core]).start()

            @pl.when(jnp.logical_not(here))
            def _():
                copy(zt.at[n, e], rb.at[k, h, core], z_send.at[n, e], z_recv.at[k, h, core], rr, ct).start()

    def sent_to_owner(n):
        for e, rr, ct in owners(n):

            @pl.when(jnp.logical_or(rr != r, ct != c))
            def _():
                pltpu.make_async_copy(zt.at[n, e], zt.at[n, e], z_send.at[n, e]).wait()

    def update(k):
        marks = jnp.concatenate(
            [jnp.sum(gat[8 * b : 8 * b + 8, :HEAD, :], axis=0)[k : k + 1, :] for b in range(S)], axis=1
        )
        for hs in range(S):
            for cs in range(2):
                arrive(rb.at[k, hs, cs], z_recv.at[k, hs, cs])
        parts = rb[k]
        total = (parts[0] + parts[1]) + (parts[2] + parts[3])
        total = jnp.concatenate([total[0], total[1]], axis=1) * marks
        col_ref[:, k, :] = total
        ch, cl = split(total)
        u = regroup(dot3(ch, cl, mh[k], ml[k]))
        for q in range(S):
            ub[k, q] = u[:, q * LANES : (q + 1) * LANES]
        for d in (2, 1, 3):
            yy = mod(y + d)
            send(ub.at[k, yy], yu.at[k, d], u_send.at[k, d], u_recv.at[k, d], rid(yy, h), c)

    def across(k):
        for d in (1, 3, 2):
            arrive(yu.at[k, d], u_recv.at[k, d])
        zv[k, h] = (ub[k, y] + yu[k, 1]) + (yu[k, 2] + yu[k, 3])
        for d in (2, 1, 3):
            send(zv.at[k, h], zv.at[k, h], v_send.at[k, d], v_recv.at[k, d], rid(y, mod(h + d)), c)

    def back(k):
        for d in (1, 3, 2):
            hs = mod(h + S - d)
            arrive(zv.at[k, hs], v_recv.at[k, d])
        fw[k, y] = (zv[k, 0] + zv[k, 1]) + (zv[k, 2] + zv[k, 3])
        for d in (2, 1, 3):
            send(fw.at[k, y], fw.at[k, y], w_send.at[k, d], w_recv.at[k, d], rid(mod(y + d), h), c)

    def finish(k):
        for d in (1, 3, 2):
            ys = mod(y + S - d)
            arrive(fw.at[k, ys], w_recv.at[k, d])
        for q in range(S):
            sch_ref[:, k, q * LANES : (q + 1) * LANES] = fw[k, q]

    start_gather(0)
    start_gather(1)
    prepare()
    line_gather(0)
    heard(0)
    start_gather(2)
    line_gather(1)
    heard(1)
    relay_gather(0)
    heard(2)
    start_gather(3)
    line_gather(2)
    heard(3)
    finish_gather(0)
    product(0)
    heard(4)
    relay_gather(1)
    line_gather(3)
    finish_gather(1)
    product(1)
    to_owner(0)
    relay_gather(2)
    finish_gather(2)
    product(2)
    to_owner(1)
    relay_gather(3)
    finish_gather(3)
    product(3)
    to_owner(2)
    to_owner(3)
    for n in range(CHUNKS):
        gathered(n)
    update(0)
    across(0)
    update(1)
    across(1)
    back(0)
    back(1)
    finish(0)
    finish(1)
    for it in sends:
        it.wait_send()
    for n in range(CHUNKS):
        sent_to_owner(n)


def local(inv_known, pattern, factor, listed, diag_inverse):
    width = diag_inverse.shape[0]
    vmem = pl.BlockSpec(memory_space=pltpu.VMEM)
    dma = pltpu.SemaphoreType.DMA
    out = jax.ShapeDtypeStruct((width, KS, 512), F32)
    sums, total = pl.pallas_call(
        kernel,
        out_shape=(out, out),
        in_specs=[pl.BlockSpec(memory_space=pl.ANY), vmem, vmem, vmem],
        out_specs=(vmem, vmem),
        scratch_shapes=[
            pltpu.VMEM((512, 256), F32),
            pltpu.VMEM((256, 512), BF16),
            pltpu.VMEM((256, 512), BF16),
            pltpu.VMEM((32, GR, LANES), F32),
            pltpu.VMEM((KS, 512, 512), BF16),
            pltpu.VMEM((KS, 512, 512), BF16),
            pltpu.VMEM((CHUNKS, S, 2, PART, 256), F32),
            pltpu.VMEM((CHUNKS, S, 2, PART, 256), F32),
            pltpu.VMEM((CHUNKS, 4, ROWS, 256), F32),
            pltpu.VMEM((KS, S, 2, ROWS, 256), F32),
            pltpu.VMEM((KS, S, ROWS, LANES), F32),
            pltpu.VMEM((KS, S, ROWS, LANES), F32),
            pltpu.VMEM((KS, S, ROWS, LANES), F32),
            pltpu.VMEM((KS, S, ROWS, LANES), F32),
            dma(()), pltpu.SemaphoreType.REGULAR((5,)),
            dma((CHUNKS,)), dma((CHUNKS, 32)),
            dma((CHUNKS, S)), dma((CHUNKS, S)),
            dma((CHUNKS, 4)), dma((KS, S, 2)),
            dma((KS, S)), dma((KS, S)),
            dma((KS, S)), dma((KS, S)),
            dma((KS, S)), dma((KS, S)),
        ],
        compiler_params=pltpu.CompilerParams(collective_id=0, has_side_effects=True),
    )(inv_known, pattern.T, factor, listed.T)
    return -sums, diag_inverse + total


def solution(mesh):
    in_specs = (
        P("row", "col"),
        P("row", "col"),
        P(("row", "col"), None, None),
        P(("row", "col"), None),
        P("col", None, None),
    )
    out_specs = (P("col", None, "row"), P("col", None, None))
    return jax.shard_map(local, mesh=mesh, in_specs=in_specs, out_specs=out_specs, check_vma=False)
```

time: 88.2 us -> 77 us (0.87)
  the two profiles are of different devices: /device:TPU:72 before, /device:TPU:70 now
where the time goes in v2:
time: 77 us; the launch traced here: 76.8 us
  Pallas kernels  74 us (96%)
  other arithmetic  2.2 us (3%)
    pallas_call x1, Pallas kernels, local(): pl.pallas_call(kernel, out_shape=(out, out), in_specs=[pl.BlockSpec(memor...  74 us

profile of v2, /device:TPU:70, one launch (start us, length us, event | category | flops | bytes accessed | tf_op | source)
XLA Modules:
  0.0 76.8 jit_solution(13708728356524084831)
XLA Ops:
  0.6 74.0 %shard_map.68 = (f32[16,2,512]{2,1,0:T(2,128)}, f32[16,2,512]{2,1,0:T(2,128)}) custom-call(f32[512,256]{1,0:T(8,128)} %inv_ref.1, s32[4,8]{1,0:T(4,128)} %bitcast.2, f32[16,2,512]{2,1,0:T(2,128)} %fac_ref.1, s32[2,16]{1,0:T(2,128)} %bitcast.3), custom_call_target="tpu_custom_call" | custom-call | tf_op jit(solution)/shard_map/pallas_call | solution.py:342
  74.6 0.0 copy-start
  74.6 0.0 copy-start.1
  74.6 1.5 %neg.3 = f32[16,2,512]{2,1,0:T(2,128)} negate(f32[16,2,512]{2,1,0:T(2,128)} %get-tuple-element.4) | non-fusion elementwise | flops 16384 | bytes 131072 | tf_op jit(solution)/shard_map/neg | solution.py:372
  76.2 0.0 copy-done
  76.2 0.0 copy-done.1
  76.2 0.7 add.3
Async XLA Ops:
  74.6 1.6 %copy-start = (f32[16,2,512]{2,1,0:T(2,128)S(1)}, f32[16,2,512]{2,1,0:T(2,128)}, u32[]{:S(2)}) copy-start(f32[16,2,512]{2,1,0:T(2,128)} %param.9) | copy-start | bytes 196612
  74.6 1.5 %copy-start.1 = (f32[16,2,512]{2,1,0:T(2,128)S(1)}, f32[16,2,512]{2,1,0:T(2,128)}, u32[]{:S(2)}) copy-start(f32[16,2,512]{2,1,0:T(2,128)} %get-tuple-element.5) | copy-start | bytes 196612

commit v3 on v2

--- a/solution.py
+++ b/solution.py
@@ -14,9 +14,11 @@
 KS = 2
 LANES = 128
 PART = 32
-CHUNKS = 4
+CUTS = (0, 1, 2, 4, 6, 8)
+CHUNKS = len(CUTS) - 1
+DIRECT = (0, 1, 2, 3, 4)
 HEAD = 8
-GR = HEAD + CHUNKS * 2 * ROWS
+GR = HEAD + KS * S * ROWS
 
 
 def mod(v):
@@ -137,8 +139,8 @@
         pltpu.make_async_copy(dst, dst, sem).wait()
 
     def span(n):
-        first = 0 if n == 0 else HEAD + n * 2 * ROWS
-        return pl.ds(first, HEAD + (n + 1) * 2 * ROWS - first)
+        first = 0 if n == 0 else HEAD + CUTS[n] * ROWS
+        return pl.ds(first, HEAD + CUTS[n + 1] * ROWS - first)
 
     def pass_on(n, cs, *to):
         shard = gat.at[cs, span(n)]
@@ -148,29 +150,32 @@
     def got(n, cs):
         arrive(gat.at[cs, span(n)], g_recv.at[n, cs])
 
+    def opposite(n):
+        return (across_x,) if n in DIRECT else ()
+
     def start_gather(n):
-        pass_on(n, c, right, left, cid(x, line[2], core), cid(x, line[1], core), cid(x, line[0], core), partner)
+        pass_on(n, c, right, left, *opposite(n), cid(x, line[2], core), cid(x, line[1], core), cid(x, line[0], core), partner)
 
     def line_gather(n):
         got(n, left)
-        pass_on(n, left, right, partner)
+        pass_on(n, left, *([] if n in DIRECT else [right]), partner)
         got(n, right)
         pass_on(n, right, partner)
         for zz in line:
             cs = cid(x, zz, core)
             got(n, cs)
-            pass_on(n, cs, right, left, partner)
+            pass_on(n, cs, right, left, *opposite(n), partner)
 
     def relay_gather(n):
         for e, zz in enumerate(line):
             cs = cid(mod(x + 3), zz, core)
             got(n, cs)
-            if e == 0:
+            if e == 0 and n not in DIRECT:
                 pass_on(n, cs, right)
             pass_on(n, cs, partner)
             cs = cid(mod(x + 1), zz, core)
             got(n, cs)
-            if e != 0:
+            if e != 0 and n not in DIRECT:
                 pass_on(n, cs, left)
             pass_on(n, cs, partner)
 
@@ -200,52 +205,55 @@
             ph[:, at] = hi
             plo[:, at] = lo
 
+    def blocks(n):
+        return range(CUTS[n], CUTS[n + 1])
+
     def product(n):
-        k, p = n // 2, n % 2
-        at = HEAD + n * 2 * ROWS
-        block = jnp.concatenate(
-            [gat[:, at + e * ROWS : at + (e + 1) * ROWS, :].reshape(32 * ROWS, LANES) for e in range(2)], axis=1
-        )
-        bh, bl = split(block)
-        mh[k, :, p * 256 : (p + 1) * 256] = bh
-        ml[k, :, p * 256 : (p + 1) * 256] = bl
+        k, p = CUTS[n] // S, CUTS[n] % S
+        cols = slice(p * LANES, p * LANES + len(blocks(n)) * LANES)
+        rows = [gat[:, HEAD + b * ROWS : HEAD + (b + 1) * ROWS, :].reshape(32 * ROWS, LANES) for b in blocks(n)]
+        bh, bl = split(jnp.concatenate(rows, axis=1))
+        mh[k, :, cols] = bh
+        ml[k, :, cols] = bl
         t = dot3(ph[...], plo[...], bh, bl).T
-        for e in range(2):
+        for e, b in enumerate(blocks(n)):
             for q in range(S):
                 at = (e * S + q) * PART
-                tq[n, q, e] = t[at : at + PART]
+                tq[q, b] = t[at : at + PART]
+        run = pl.ds(CUTS[n], len(blocks(n)))
         for d in (2, 1, 3):
             yy = mod(y + d)
-            send(tq.at[n, quarter(x, yy)], yb.at[n, d], y_send.at[n, d], y_recv.at[n, d], rid(yy, h), c)
+            send(tq.at[quarter(x, yy), run], yb.at[d, run], y_send.at[n, d], y_recv.at[n, d], rid(yy, h), c)
 
     def owners(n):
-        for e in range(2):
+        for b in blocks(n):
             for cc in range(2):
-                yield e * 2 + cc, rid(x, z), cid(mine, (n % 2) * 2 + e, cc)
+                yield b, cc, rid(x, z), cid(mine, b % S, cc)
 
     def to_owner(n):
-        k = n // 2
+        run = pl.ds(CUTS[n], len(blocks(n)))
         for d in (1, 3, 2):
-            arrive(yb.at[n, d], y_recv.at[n, d])
-        total = (tq[n, mine] + yb[n, 1]) + (yb[n, 2] + yb[n, 3])
-        zt[n] = total.reshape(4, ROWS, 256)
-        for e, rr, ct in owners(n):
+            arrive(yb.at[d, run], y_recv.at[n, d])
+        total = (tq[mine, run] + yb[1, run]) + (yb[2, run] + yb[3, run])
+        zt[run] = total.reshape(len(blocks(n)), 2, ROWS, 256)
+        for b, e, rr, ct in owners(n):
+            k = b // S
             here = jnp.logical_and(rr == r, ct == c)
 
             @pl.when(here)
             def _():
-                pltpu.make_async_copy(zt.at[n, e], rb.at[k, h, core], z_recv.at[k, h, core]).start()
+                pltpu.make_async_copy(zt.at[b, e], rb.at[k, h, core], z_recv.at[k, h, core]).start()
 
             @pl.when(jnp.logical_not(here))
             def _():
-                copy(zt.at[n, e], rb.at[k, h, core], z_send.at[n, e], z_recv.at[k, h, core], rr, ct).start()
+                copy(zt.at[b, e], rb.at[k, h, core], z_send.at[b, e], z_recv.at[k, h, core], rr, ct).start()
 
     def sent_to_owner(n):
-        for e, rr, ct in owners(n):
+        for b, e, rr, ct in owners(n):
 
             @pl.when(jnp.logical_or(rr != r, ct != c))
             def _():
-                pltpu.make_async_copy(zt.at[n, e], zt.at[n, e], z_send.at[n, e]).wait()
+                pltpu.make_async_copy(zt.at[b, e], zt.at[b, e], z_send.at[b, e]).wait()
 
     def update(k):
         marks = jnp.concatenate(
@@ -290,34 +298,40 @@
 
     start_gather(0)
     start_gather(1)
+    start_gather(2)
+    start_gather(3)
+    start_gather(4)
     prepare()
     line_gather(0)
     heard(0)
-    start_gather(2)
     line_gather(1)
     heard(1)
+    line_gather(2)
+    heard(2)
+    line_gather(3)
+    heard(3)
+    line_gather(4)
     relay_gather(0)
-    heard(2)
-    start_gather(3)
-    line_gather(2)
-    heard(3)
     finish_gather(0)
+    heard(4)
     product(0)
-    heard(4)
     relay_gather(1)
-    line_gather(3)
     finish_gather(1)
     product(1)
-    to_owner(0)
     relay_gather(2)
     finish_gather(2)
     product(2)
-    to_owner(1)
     relay_gather(3)
     finish_gather(3)
     product(3)
+    to_owner(0)
+    to_owner(1)
+    relay_gather(4)
+    finish_gather(4)
+    product(4)
     to_owner(2)
     to_owner(3)
+    to_owner(4)
     for n in range(CHUNKS):
         gathered(n)
     update(0)
@@ -351,9 +365,9 @@
             pltpu.VMEM((32, GR, LANES), F32),
             pltpu.VMEM((KS, 512, 512), BF16),
             pltpu.VMEM((KS, 512, 512), BF16),
-            pltpu.VMEM((CHUNKS, S, 2, PART, 256), F32),
-            pltpu.VMEM((CHUNKS, S, 2, PART, 256), F32),
-            pltpu.VMEM((CHUNKS, 4, ROWS, 256), F32),
+            pltpu.VMEM((S, KS * S, PART, 256), F32),
+            pltpu.VMEM((S, KS * S, PART, 256), F32),
+            pltpu.VMEM((KS * S, 2, ROWS, 256), F32),
             pltpu.VMEM((KS, S, 2, ROWS, 256), F32),
             pltpu.VMEM((KS, S, ROWS, LANES), F32),
             pltpu.VMEM((KS, S, ROWS, LANES), F32),
@@ -362,7 +376,7 @@
             dma(()), pltpu.SemaphoreType.REGULAR((5,)),
             dma((CHUNKS,)), dma((CHUNKS, 32)),
             dma((CHUNKS, S)), dma((CHUNKS, S)),
-            dma((CHUNKS, 4)), dma((KS, S, 2)),
+            dma((KS * S, 2)), dma((KS, S, 2)),
             dma((KS, S)), dma((KS, S)),
             dma((KS, S)), dma((KS, S)),
             dma((KS, S)), dma((KS, S)),

time: 77 us -> 69.4 us (0.901)
  the two profiles are of different devices: /device:TPU:70 before, /device:TPU:102 now
where the time goes in v3:
time: 69.4 us; the launch traced here: 69.2 us
  Pallas kernels  66.3 us (96%)
  other arithmetic  2.2 us (3%)
    pallas_call x1, Pallas kernels, local(): pl.pallas_call(kernel, out_shape=(out, out), in_specs=[pl.BlockSpec(memor...  66.3 us
    neg x1, other arithmetic, local(): return (-sums, diag_inverse + total)  1.53 us

profile of v3, /device:TPU:102, one launch (start us, length us, event | category | flops | bytes accessed | tf_op | source)
XLA Modules:
  0.0 69.2 jit_solution(5084946919966439175)
XLA Ops:
  0.6 66.3 %shard_map.68 = (f32[16,2,512]{2,1,0:T(2,128)}, f32[16,2,512]{2,1,0:T(2,128)}) custom-call(f32[512,256]{1,0:T(8,128)} %inv_ref.1, s32[4,8]{1,0:T(4,128)} %bitcast.2, f32[16,2,512]{2,1,0:T(2,128)} %fac_ref.1, s32[2,16]{1,0:T(2,128)} %bitcast.3), custom_call_target="tpu_custom_call" | custom-call | tf_op jit(solution)/shard_map/pallas_call | solution.py:356
  67.0 0.0 copy-start
  67.0 0.0 copy-start.1
  67.0 1.5 %neg.3 = f32[16,2,512]{2,1,0:T(2,128)} negate(f32[16,2,512]{2,1,0:T(2,128)} %get-tuple-element.4) | non-fusion elementwise | flops 16384 | bytes 131072 | tf_op jit(solution)/shard_map/neg | solution.py:386
  68.5 0.0 copy-done
  68.5 0.0 copy-done.1
  68.5 0.7 add.3
Async XLA Ops:
  67.0 1.6 %copy-start = (f32[16,2,512]{2,1,0:T(2,128)S(1)}, f32[16,2,512]{2,1,0:T(2,128)}, u32[]{:S(2)}) copy-start(f32[16,2,512]{2,1,0:T(2,128)} %param.9) | copy-start | bytes 196612
  67.0 1.5 %copy-start.1 = (f32[16,2,512]{2,1,0:T(2,128)S(1)}, f32[16,2,512]{2,1,0:T(2,128)}, u32[]{:S(2)}) copy-start(f32[16,2,512]{2,1,0:T(2,128)} %get-tuple-element.5) | copy-start | bytes 196612

commit v4 on v3

--- a/solution.py
+++ b/solution.py
@@ -16,7 +16,7 @@
 PART = 32
 CUTS = (0, 1, 2, 4, 6, 8)
 CHUNKS = len(CUTS) - 1
-DIRECT = (0, 1, 2, 3, 4)
+ROUND = ()
 HEAD = 8
 GR = HEAD + KS * S * ROWS
 
@@ -45,8 +45,8 @@
 
 
 def kernel(
-    inv_ref, pat_ref, fac_ref, lst_ref, col_ref, sch_ref,
-    inv, ph, plo, gat, mh, ml, tq, yb, zt, rb, ub, yu, zv, fw,
+    inv_in, pat_in, fac_in, lst_in, col_ref, sch_ref,
+    inv, pat_ref, fac_ref, lst_ref, ph, plo, gat, mh, ml, tq, yb, zt, rb, ub, yu, zv, fw,
     i_sem, far_sem, g_send, g_recv, y_send, y_recv, z_send, z_recv,
     u_send, u_recv, v_send, v_recv, w_send, w_recv,
 ):
@@ -83,8 +83,16 @@
     for cc in (right, left, across_x, partner):
         greet(barrier, r, cc)
 
-    load = pltpu.make_async_copy(inv_ref, inv, i_sem)
+    small = [
+        pltpu.make_async_copy(src, dst, i_sem.at[e])
+        for e, (src, dst) in enumerate([(fac_in, fac_ref), (lst_in, lst_ref), (pat_in, pat_ref)])
+    ]
+    for it in small:
+        it.start()
+    load = pltpu.make_async_copy(inv_in, inv, i_sem.at[3])
     load.start()
+    for it in small[:2]:
+        it.wait()
 
     listed = lst_ref[...].astype(F32)
     eye = lax.broadcasted_iota(jnp.int32, (ROWS, ROWS), 0) == lax.broadcasted_iota(jnp.int32, (ROWS, ROWS), 1)
@@ -150,37 +158,38 @@
     def got(n, cs):
         arrive(gat.at[cs, span(n)], g_recv.at[n, cs])
 
-    def opposite(n):
-        return (across_x,) if n in DIRECT else ()
-
     def start_gather(n):
-        pass_on(n, c, right, left, *opposite(n), cid(x, line[2], core), cid(x, line[1], core), cid(x, line[0], core), partner)
+        pass_on(n, c, right, left, across_x, cid(x, line[2], core), cid(x, line[1], core), cid(x, line[0], core), partner)
 
     def line_gather(n):
-        got(n, left)
-        pass_on(n, left, *([] if n in DIRECT else [right]), partner)
-        got(n, right)
-        pass_on(n, right, partner)
+        lines = [cid(x, zz, core) for zz in line]
+        rings = [left, right, across_x]
+        if n in ROUND:
+            for cs in rings:
+                got(n, cs)
+                pass_on(n, cs, *lines, partner)
+            for cs in lines:
+                got(n, cs)
+                pass_on(n, cs, partner)
+        else:
+            for cs in rings[:2]:
+                got(n, cs)
+                pass_on(n, cs, partner)
+            for cs in lines:
+                got(n, cs)
+                pass_on(n, cs, *rings, partner)
+            got(n, across_x)
+            pass_on(n, across_x, partner)
+
+    def relay_gather(n):
         for zz in line:
-            cs = cid(x, zz, core)
-            got(n, cs)
-            pass_on(n, cs, right, left, *opposite(n), partner)
-
-    def relay_gather(n):
-        for e, zz in enumerate(line):
-            cs = cid(mod(x + 3), zz, core)
-            got(n, cs)
-            if e == 0 and n not in DIRECT:
-                pass_on(n, cs, right)
-            pass_on(n, cs, partner)
-            cs = cid(mod(x + 1), zz, core)
-            got(n, cs)
-            if e != 0 and n not in DIRECT:
-                pass_on(n, cs, left)
-            pass_on(n, cs, partner)
+            for d in (3, 1):
+                cs = cid(mod(x + d), zz, core)
+                got(n, cs)
+                pass_on(n, cs, partner)
 
     def finish_gather(n):
-        for zz in (z, *line):
+        for zz in line:
             cs = cid(mod(x + 2), zz, core)
             got(n, cs)
             pass_on(n, cs, partner)
@@ -192,6 +201,7 @@
         pltpu.make_async_copy(shards, shards, g_send.at[n]).wait()
 
     def prepare():
+        small[2].wait()
         flags = pat_ref[...].astype(F32)
         tile = lax.div(lax.broadcasted_iota(jnp.int32, (S, 512), 1), 64)
         wide = jnp.zeros((S, 512), F32)
@@ -267,7 +277,8 @@
         total = jnp.concatenate([total[0], total[1]], axis=1) * marks
         col_ref[:, k, :] = total
         ch, cl = split(total)
-        u = regroup(dot3(ch, cl, mh[k], ml[k]))
+        both = jnp.dot(jnp.concatenate([ch, cl], axis=0), mh[k], preferred_element_type=F32)
+        u = regroup(both[:ROWS] + (both[ROWS:] + jnp.dot(ch, ml[k], preferred_element_type=F32)))
         for q in range(S):
             ub[k, q] = u[:, q * LANES : (q + 1) * LANES]
         for d in (2, 1, 3):
@@ -356,10 +367,13 @@
     sums, total = pl.pallas_call(
         kernel,
         out_shape=(out, out),
-        in_specs=[pl.BlockSpec(memory_space=pl.ANY), vmem, vmem, vmem],
+        in_specs=[pl.BlockSpec(memory_space=pl.ANY)] * 4,
         out_specs=(vmem, vmem),
         scratch_shapes=[
             pltpu.VMEM((512, 256), F32),
+            pltpu.VMEM((S, 8), jnp.int32),
+            pltpu.VMEM((ROWS, KS, 512), F32),
+            pltpu.VMEM((KS, ROWS), jnp.int32),
             pltpu.VMEM((256, 512), BF16),
             pltpu.VMEM((256, 512), BF16),
             pltpu.VMEM((32, GR, LANES), F32),
@@ -373,7 +387,7 @@
             pltpu.VMEM((KS, S, ROWS, LANES), F32),
             pltpu.VMEM((KS, S, ROWS, LANES), F32),
             pltpu.VMEM((KS, S, ROWS, LANES), F32),
-            dma(()), pltpu.SemaphoreType.REGULAR((5,)),
+            dma((4,)), pltpu.SemaphoreType.REGULAR((5,)),
             dma((CHUNKS,)), dma((CHUNKS, 32)),
             dma((CHUNKS, S)), dma((CHUNKS, S)),
             dma((KS * S, 2)), dma((KS, S, 2)),
@@ -383,7 +397,14 @@
         ],
         compiler_params=pltpu.CompilerParams(collective_id=0, has_side_effects=True),
     )(inv_known, pattern.T, factor, listed.T)
-    return -sums, diag_inverse + total
+
+    def close(sums_ref, total_ref, dia_ref, col_ref, sch_ref):
+        col_ref[...] = -sums_ref[...]
+        sch_ref[...] = dia_ref[...] + total_ref[...]
+
+    return pl.pallas_call(close, out_shape=(out, out), in_specs=[vmem] * 3, out_specs=(vmem, vmem))(
+        sums, total, diag_inverse
+    )
 
 
 def solution(mesh):

time: 69.4 us -> 68 us (0.980)
  other arithmetic: 2.2 us -> 0 us
  Pallas kernels: 66.3 us -> 67.2 us
    pallas_call x0 -> x1, Pallas kernels: none -> 1.56 us  [local(): pl.pallas_call(close, out_shape=(out, out), in_specs=[vmem] * 3, out_spec...]
    neg x1 -> x0, other arithmetic: 1.53 us -> none  [local(): return (-sums, diag_inverse + total)]
where the time goes in v4:
time: 68 us; the launch traced here: 67.9 us
  Pallas kernels  67.2 us (99%)
    pallas_call x1, Pallas kernels, local(): pl.pallas_call(kernel, out_shape=(out, out), in_specs=[pl.BlockSpec(memor...  65.7 us
    pallas_call x1, Pallas kernels, local(): pl.pallas_call(close, out_shape=(out, out), in_specs=[vmem] * 3, out_spec...  1.56 us

profile of v4, /device:TPU:102, one launch (start us, length us, event | category | flops | bytes accessed | tf_op | source)
XLA Modules:
  0.0 67.9 jit_solution(6630209133503038454)
XLA Ops:
  0.6 65.7 %shard_map.68 = (f32[16,2,512]{2,1,0:T(2,128)}, f32[16,2,512]{2,1,0:T(2,128)}) custom-call(f32[512,256]{1,0:T(8,128)} %inv_in.1, s32[4,8]{1,0:T(4,128)} %bitcast.2, f32[16,2,512]{2,1,0:T(2,128)} %fac_in.1, s32[2,16]{1,0:T(2,128)} %bitcast.3), custom_call_target="tpu_custom_call" | custom-call | tf_op jit(solution)/shard_map/pallas_call | solution.py:367
  66.3 1.6 %shard_map.69 = (f32[16,2,512]{2,1,0:T(2,128)}, f32[16,2,512]{2,1,0:T(2,128)}) custom-call(f32[16,2,512]{2,1,0:T(2,128)} %get-tuple-element.4.sums_ref, f32[16,2,512]{2,1,0:T(2,128)} %get-tuple-element.5.total_ref, f32[16,2,512]{2,1,0:T(2,128)} %dia_ref.1), custom_call_target="tpu_custom_call" | custom-call | tf_op jit(solution)/shard_map/pallas_call | solution.py:405

commit v5 on v4

--- a/solution.py
+++ b/solution.py
@@ -312,7 +312,6 @@
     start_gather(2)
     start_gather(3)
     start_gather(4)
-    prepare()
     line_gather(0)
     heard(0)
     line_gather(1)
@@ -322,6 +321,7 @@
     line_gather(3)
     heard(3)
     line_gather(4)
+    prepare()
     relay_gather(0)
     finish_gather(0)
     heard(4)
@@ -335,16 +335,14 @@
     relay_gather(3)
     finish_gather(3)
     product(3)
+    relay_gather(4)
     to_owner(0)
     to_owner(1)
-    relay_gather(4)
     finish_gather(4)
     product(4)
     to_owner(2)
     to_owner(3)
     to_owner(4)
-    for n in range(CHUNKS):
-        gathered(n)
     update(0)
     across(0)
     update(1)
@@ -353,6 +351,8 @@
     back(1)
     finish(0)
     finish(1)
+    for n in range(CHUNKS):
+        gathered(n)
     for it in sends:
         it.wait_send()
     for n in range(CHUNKS):

time: 68 us -> 68 us (level)
  no operation moved by 1% of the time
where the time goes in v5:
time: 68 us; the launch traced here: 67.9 us
  Pallas kernels  67.2 us (99%)
    pallas_call x1, Pallas kernels, local(): pl.pallas_call(kernel, out_shape=(out, out), in_specs=[pl.BlockSpec(memor...  65.7 us
    pallas_call x1, Pallas kernels, local(): pl.pallas_call(close, out_shape=(out, out), in_specs=[vmem] * 3, out_spec...  1.56 us

profile of v5, /device:TPU:102, one launch (start us, length us, event | category | flops | bytes accessed | tf_op | source)
XLA Modules:
  0.0 67.9 jit_solution(4592244713988975559)
XLA Ops:
  0.6 65.7 %shard_map.68 = (f32[16,2,512]{2,1,0:T(2,128)}, f32[16,2,512]{2,1,0:T(2,128)}) custom-call(f32[512,256]{1,0:T(8,128)} %inv_in.1, s32[4,8]{1,0:T(4,128)} %bitcast.2, f32[16,2,512]{2,1,0:T(2,128)} %fac_in.1, s32[2,16]{1,0:T(2,128)} %bitcast.3), custom_call_target="tpu_custom_call" | custom-call | tf_op jit(solution)/shard_map/pallas_call | solution.py:367
  66.3 1.6 %shard_map.69 = (f32[16,2,512]{2,1,0:T(2,128)}, f32[16,2,512]{2,1,0:T(2,128)}) custom-call(f32[16,2,512]{2,1,0:T(2,128)} %get-tuple-element.4.sums_ref, f32[16,2,512]{2,1,0:T(2,128)} %get-tuple-element.5.total_ref, f32[16,2,512]{2,1,0:T(2,128)} %dia_ref.1), custom_call_target="tpu_custom_call" | custom-call | tf_op jit(solution)/shard_map/pallas_call | solution.py:405
